TPU v7x, 1024 devices: a whole 4x8x16 slice. The times are simulated.
1024 devices in a mesh: vir: 128 (over z_hi, x, y, core), out: 8 (over z_lo).
Axes of the slice: x: 4, y: 8, z: 16 (z_hi: 2, z_lo: 8; z = z_hi * 8 + z_lo), core: 2. Of those that a mesh axis runs over, the one named last changes fastest.
Arguments:
- factors: bfloat16 [512, 512, 1536], P('out', 'vir'), may hold values from -2.5 to 2.5
- amplitudes: bfloat16 [128, 512, 512], P('out', 'vir'), may hold values from -0.046875 to 0.046875
Outputs:
- ladder: float32 [2, 128, 512], P(None, 'vir', 'out')
All inputs are finite; a program needn't handle non-finite values.
Results may differ from a plain program's by a relative error of at most 0.0029.
Values may be sent and summed in bfloat16 or wider, within the bound.
A program may use at most 32 MiB of HBM per device.

v0:
```python
import jax
import jax.numpy as jnp
from jax import lax
from jax.sharding import Mesh
from jax.sharding import PartitionSpec as P

BB = 2
VIR = ("vir_0", "vir_1", "vir_2", "vir_3")


def sent_to_all(x, axis):
    copies = jnp.broadcast_to(x, (lax.axis_size(axis), *x.shape))
    return lax.all_to_all(copies, axis, split_axis=0, concat_axis=0, tiled=True)


def laid_out(blocks, dim):
    dims = list(blocks.shape[1:])
    dims[dim] *= blocks.shape[0]
    return jnp.moveaxis(blocks, 0, dim).reshape(dims)


def collect(x, axis, dim):
    blocks = sent_to_all(x, axis)
    return laid_out(blocks, dim)


def picked(x, axis, root):
    return lax.dynamic_index_in_dim(lax.all_gather(x, axis), root, 0, keepdims=False)


def in_blocks(x, dim, peers):
    before, after = (x.shape[:dim], x.shape[dim + 1 :])
    return jnp.moveaxis(x.reshape(*before, peers, -1, *after), dim, 0)


def sum_by_chip(x, chips, core, dim):
    sizes = (lax.axis_size(chips), lax.axis_size(core))
    blocks = in_blocks(x, dim, sizes[0] * sizes[1])
    inside = blocks.shape[1:]
    blocks = blocks.reshape(*sizes, *inside).swapaxes(0, 1).reshape(-1, *inside)
    blocks = lax.psum_scatter(blocks, core, scatter_dimension=0, tiled=True)
    return lax.psum_scatter(blocks, chips, scatter_dimension=0, tiled=True)[0]


def body(factors, amplitudes):
    a_rows, c_rows, aux_len = factors.shape
    local_rows = factors.reshape(a_rows * c_rows, aux_len)
    every_pair = collect(amplitudes, "out", 0)
    batch_rows = factors[:BB]
    shared = picked(batch_rows, "out", 0)
    gathered = lax.all_gather(shared, VIR, axis=1, tiled=True)
    piece_len = gathered.shape[1]
    tiles = lax.dot_general(
        local_rows, gathered, (((1,), (2,)), ((), ())), preferred_element_type=jnp.float32
    )
    integral = tiles.astype(jnp.bfloat16).reshape(a_rows, c_rows, BB, piece_len)
    terms = jnp.einsum("acbd,pcd->bpa", integral, every_pair, preferred_element_type=jnp.float32)
    return sum_by_chip(terms, ("vir_0", "vir_1", "vir_2"), "vir_3", 1)


def solution(mesh):
    torus = Mesh(
        mesh.devices.reshape(2, 4, 8, 2, mesh.shape["out"]),
        ("vir_0", "vir_1", "vir_2", "vir_3", "out"),
    )
    in_specs = (P("out", VIR, None), P("out", VIR, None))
    out_specs = P(None, VIR, "out")
    return jax.shard_map(body, mesh=torus, in_specs=in_specs, out_specs=out_specs, check_vma=False)
```

profile of v0, /device:TPU:64, one launch (start us, length us, event | category | flops | bytes accessed | tf_op | source)
XLA Modules:
  0.0 853.1 jit_solution(15770951485762231026)
XLA Ops:
  6.5 0.0 all-gather.5.cloned.1.call-start
  6.5 0.7 slice.4
  7.3 52.1 %all-gather = bf16[16,4,1536]{2,1,0:T(4,128)(2,1)S(1)} all-gather(bf16[2,4,1536]{2,1,0:T(4,128)(2,1)S(1)} %slice.4), channel_id=2, replica_groups=mesh['vir_0'=2,'vir_1'=4,'vir_2'=8,'vir_3'=2,'out'=8] {'out'}, dimensions={0}, use_global_device_ids=true | all-gather | bytes 221184 | tf_op jit(solution)/shard_map/all_gather | solution.py:28
  59.4 0.6 copy.21
  60.0 0.0 all-gather.5.cloned.1.call-update
  60.1 0.9 copy.23
  60.9 0.9 broadcast_in_dim.3
  61.8 10.1 %all-to-all-start = ((bf16[8,16,4,512]{3,1,2,0:T(8,128)(2,1)}), bf16[8,16,4,512]{3,1,2,0:T(8,128)(2,1)S(1)}, u32[]{:S(2)}, u32[]{:S(2)}) async-start(bf16[8,16,4,512]{3,1,2,0:T(8,128)(2,1)} %broadcast_in_dim.3), calls=%async_computation | async-start | bytes 1048576 | tf_op jit(solution)/shard_map/all_to_all | solution.py:13
  71.9 0.0 reduce-scatter.4.cloned.1.call-start
  71.9 1.6 reshape.29
  73.4 18.7 %all-to-all-done = bf16[8,16,4,512]{3,1,2,0:T(8,128)(2,1)S(1)} async-done(((bf16[8,16,4,512]{3,1,2,0:T(8,128)(2,1)}), bf16[8,16,4,512]{3,1,2,0:T(8,128)(2,1)S(1)}, u32[]{:S(2)}, u32[]{:S(2)}) %all-to-all-start) | async-done | bytes 524320 | tf_op jit(solution)/shard_map/all_to_all | solution.py:13
  92.2 141.0 %all-gather.5.cloned.1.call-done = bf16[2,512,1536]{2,0,1:T(2,128)(2,1)} async-done(((bf16[2,4,1536]{2,0,1:T(2,128)(2,1)}), bf16[2,512,1536]{2,0,1:T(2,128)(2,1)}) %all-gather.5.cloned.1.call-update) | async-done | bytes 3145744 | tf_op jit(solution)/shard_map/all_gather | solution.py:51
  233.2 2.9 fusion.2
  236.1 0.1 reshape.19
  236.2 0.3 convolution_bitcast_fusion
  236.5 0.1 copy.26
  236.6 0.1 copy.33
  236.7 0.7 reshape.33
  237.5 0.0 reduce-scatter.4.cloned.1.call-update
  237.5 1.3 dynamic-slice
  238.9 8.5 reduce-scatter.4.cloned.1.call-done
  247.4 0.9 reshape.34
  248.2 596.8 %all-reduce = f32[64,2,1,64]{3,1,2,0:T(2,128)S(1)} all-reduce(f32[64,2,1,64]{3,1,2,0:T(2,128)S(1)} %bitcast.31), channel_id=6, replica_groups=mesh['vir_0'=2,'vir_1'=4,'vir_2'=8,'vir_3'=2,'out'=8] {'vir_0','vir_1','..., use_global_device_ids=true, to_apply=%region_1.2.clone | all-reduce | flops 8192 | bytes 65536
  845.0 1.2 constant_dynamic-slice_fusion
  (2 shorter events, 0.0 us)
Async XLA Ops:
  6.5 226.6 %all-gather.5.cloned.1.call-start = ((), (), s32[]{:S(2)}) async-start(), calls=%async_computation.2 | async-start | bytes 3170304 | tf_op jit(solution)/shard_map/all_gather | solution.py:51
  61.8 30.4 %all-to-all-start = ((bf16[8,16,4,512]{3,1,2,0:T(8,128)(2,1)}), bf16[8,16,4,512]{3,1,2,0:T(8,128)(2,1)S(1)}, u32[]{:S(2)}, u32[]{:S(2)}) async-start(bf16[8,16,4,512]{3,1,2,0:T(8,128)(2,1)} %broadcast_in_dim.3), calls=%async_computation | async-start | bytes 1048576 | tf_op jit(solution)/shard_map/all_to_all | solution.py:13
  71.9 175.5 %reduce-scatter.4.cloned.1.call-start = ((), (), s32[]{:S(2)}) async-start(), calls=%async_computation.3 | async-start | bytes 98304
Sparse Core Ops, SparseCore 0:
  60.2 172.9 all-gather.4
  237.6 9.7 reduce-scatter.3
where the time goes:
time: 854 us; the launch traced here: 853 us
  blocking collectives  649 us (76%)
  waiting for transfers between devices  168 us (20%)
  between operations  13.5 us (2%)
  starting transfers between devices  10.1 us (1%)
  local copies, waits for them, and re-layouts  9.21 us (1%)
    unnamed x1, blocking collectives  597 us
    all_gather x1, waiting for transfers between devices, body(): gathered = lax.all_gather(shared, VIR, axis=1, tiled=True)  141 us
    all_gather x1, blocking collectives, picked(): lax.all_gather(x, axis)  52.1 us
    all_to_all x1, waiting for transfers between devices, sent_to_all(): return lax.all_to_all(copies, axis, split_axis=0, concat_axis=0, tiled=True)  18.7 us
  transfers between devices with their start and end apart: 3, of which 3 were waited for; matrix products, arithmetic and copies ran while one was open for 1% of the time, Pallas kernels for 0%

commit v1 on v0

v1 whole, which is shorter than its diff:
```python
import jax
import jax.numpy as jnp
from jax import lax
from jax.experimental import pallas as pl
from jax.experimental.pallas import tpu as pltpu
from jax.sharding import Mesh
from jax.sharding import PartitionSpec as P

ZH, X, Y, CORE, ZL = "vir_0", "vir_1", "vir_2", "vir_3", "out"
VIR = (ZH, X, Y, CORE)
NZH, NX, NY, NC, NZL = 2, 4, 8, 2, 8
BB, NCV, NA, AUX, V, PAIRS = 2, 4, 64, 1536, 512, 128
MESH = pl.DeviceIdType.MESH
BF, F32 = jnp.bfloat16, jnp.float32


def kernel(
    f_ref, t_ref, o_ref,
    piece, slab, traw, fm, tm, te, integ, r0, ra, rbs, rb,
    local_sem, z_send, z_recv, t_send, t_recv, xn_send, xn_recv, yr_send, yr_recv,
    yf_send, yf_recv, xf_send, xf_recv, pn_send, pn_recv, pf_send, pf_recv,
    ra_send, ra_recv, rb_send, rb_recv,
):
    zh, x, y, h, zl = (lax.axis_index(n) for n in (ZH, X, Y, CORE, ZL))
    near = jnp.where(zl <= NZL // 2, zh, 1 - zh)
    sends = []

    def put(src, dst, ssem, rsem, **where):
        copy = pltpu.make_async_remote_copy(
            src_ref=src, dst_ref=dst, send_sem=ssem, recv_sem=rsem,
            device_id={names[k]: v for k, v in where.items()}, device_id_type=MESH,
        )
        copy.start()
        return copy

    names = {"zh": ZH, "x": X, "y": Y, "h": CORE, "zl": ZL}

    def arrived(dst, rsem):
        pltpu.make_async_copy(dst, dst, rsem).wait()

    def left(src, ssem):
        pltpu.make_async_copy(src, src, ssem).wait()

    barrier = pltpu.get_barrier_semaphore()

    def greet(**where):
        pl.semaphore_signal(
            barrier, inc=1, device_id={names[k]: v for k, v in where.items()}, device_id_type=MESH
        )

    idx_z = zh * NZL + zl
    for o in range(1, 16):
        other = lax.rem(idx_z + o, 16)
        greet(zh=other // NZL, zl=lax.rem(other, NZL))
    idx_a = h * NX + x
    for o in range(1, 8):
        other = lax.rem(idx_a + o, 8)
        greet(h=other // NX, x=lax.rem(other, NX))
    for o in range(1, NY):
        greet(y=lax.rem(y + o, NY))

    piece[0:4, :] = f_ref[0]
    piece[4:8, :] = f_ref[1]
    for c in range(NCV):
        fm[c * NA : (c + 1) * NA, :] = f_ref[:, c, :]

    pl.semaphore_wait(barrier, 15 + 7 + 7)

    def z_place(n):
        group = jnp.where(n == 0, 7, NZL + y // 4)
        inner = jnp.where(n == 0, x, lax.rem(y, 4))
        return slab.at[group, inner, h]

    @pl.when(zl == 0)
    def _():
        pltpu.make_async_copy(piece, z_place(0), local_sem.at[0]).start()
        for o in (8, 7, 9, 6, 10, 5, 11, 4, 12, 3, 13, 2, 14, 1, 15):
            other = lax.rem(idx_z + o, 16)
            ozh, ozl = other // NZL, lax.rem(other, NZL)
            onear = jnp.where(ozl <= NZL // 2, ozh, 1 - ozh)
            n = jnp.where(onear == zh, 0, 1)
            put(piece, z_place(n), z_send.at[o - 1], z_recv.at[n], zh=ozh, zl=ozl)
        pltpu.make_async_copy(piece, z_place(0), local_sem.at[0]).wait()

    @pl.when(zl != 0)
    def _():
        arrived(piece, z_recv.at[0])

    for o in range(1, NX):
        put(slab.at[7, x, h], slab.at[7, x, h], xn_send.at[o - 1], xn_recv.at[o - 1], x=lax.rem(x + o, NX))
    for o in range(1, NX):
        arrived(slab.at[7, x, h], xn_recv.at[o - 1])

    up, down = lax.rem(y + 1, NY), lax.rem(y + NY - 1, NY)

    def near_part(pos):
        return slab.at[pos, :, h]

    def ring(k, src, up_pos, down_pos):
        put(near_part(src[0]), near_part(up_pos), yr_send.at[2 * k], yr_recv.at[up_pos], y=up)
        put(near_part(src[1]), near_part(down_pos), yr_send.at[2 * k + 1], yr_recv.at[down_pos], y=down)

    def share_near(pos):
        put(near_part(pos), near_part(pos), pn_send.at[pos], pn_recv.at[pos], h=1 - h)

    ring(0, (7, 7), 0, 1)
    share_near(7)

    arrived(piece, z_recv.at[1])
    far = slab.at[NZL + y // 4, lax.rem(y, 4), h]
    for o in (4, 3, 5, 2, 6, 1, 7):
        put(far, far, yf_send.at[o - 1], yf_recv.at[o - 1], y=lax.rem(y + o, NY))

    pltpu.make_async_copy(t_ref, traw.at[zl], local_sem.at[0]).start()
    for o in range(1, NZL):
        put(t_ref, traw.at[zl], t_send.at[o - 1], t_recv.at[o - 1], zl=lax.rem(zl + o, NZL))
    pltpu.make_async_copy(t_ref, traw.at[zl], local_sem.at[0]).wait()

    def multiply(g):
        rows = slab[2 * g : 2 * g + 2].reshape(128, AUX)
        tile = lax.dot_general(fm[...], rows, (((1,), (1,)), ((), ())), preferred_element_type=F32)
        integ[:, g * 128 : (g + 1) * 128] = tile.astype(BF)

    for pos in (0, 1):
        arrived(near_part(pos), yr_recv.at[pos])
    ring(1, (0, 1), 2, 3)
    share_near(0)
    share_near(1)

    def far_part(k):
        return slab.at[NZL + 2 * k : NZL + 2 * k + 2, :, h]

    for o in range(1, NY):
        arrived(far, yf_recv.at[o - 1])
    for o in (2, 1, 3):
        k = NX - o
        put(far_part(0), far_part(k), xf_send.at[o - 1], xf_recv.at[k - 1], x=lax.rem(x + o, NX))
    put(far_part(0), far_part(0), pf_send.at[0], pf_recv.at[0], h=1 - h)

    for pos in (2, 3):
        arrived(near_part(pos), yr_recv.at[pos])
    ring(2, (2, 3), 4, 5)
    share_near(2)
    share_near(3)

    for pos in (4, 5):
        arrived(near_part(pos), yr_recv.at[pos])
    put(slab.at[4, 0:2, h], slab.at[6, 0:2, h], yr_send.at[6], yr_recv.at[6], y=up)
    put(slab.at[5, 2:4, h], slab.at[6, 2:4, h], yr_send.at[7], yr_recv.at[7], y=down)
    share_near(4)
    share_near(5)

    for pos in (0, 1):
        arrived(near_part(pos), pn_recv.at[pos])
    multiply(0)
    for pos in (2, 3):
        arrived(near_part(pos), pn_recv.at[pos])
    multiply(1)
    arrived(slab.at[6, 0:2, h], yr_recv.at[6])
    arrived(slab.at[6, 2:4, h], yr_recv.at[7])
    share_near(6)
    for pos in (4, 5):
        arrived(near_part(pos), pn_recv.at[pos])
    multiply(2)
    arrived(far_part(0), pf_recv.at[0])
    multiply(4)
    for k in (1, 3, 2):
        arrived(far_part(k), xf_recv.at[k - 1])
        put(far_part(k), far_part(k), pf_send.at[k], pf_recv.at[k], h=1 - h)
    for pos in (6, 7):
        arrived(near_part(pos), pn_recv.at[pos])
    multiply(3)

    for o in range(1, NZL):
        arrived(t_ref, t_recv.at[o - 1])
    for s in range(NZL):
        szh, sx = s // NX, s % NX
        for core in range(NC):
            for c in range(NCV):
                row = c * 128 + core * 64 + sx * 16 + szh * 8
                tm[row : row + 8, :] = traw[s, :, core, c, :]
    for g in range(8):
        j = lax.broadcasted_iota(jnp.int32, (V, 128), 1) + g * 128
        d = lax.broadcasted_iota(jnp.int32, (V, 128), 0)
        pos, xx, core, b, i = j // 64, (j // 16) % 4, (j // 8) % 2, (j // 4) % 2, j % 4
        if g < 4:
            step = jnp.where(pos % 2 == 0, NY - 1 - pos // 2, pos // 2 + 1)
            yy = lax.rem(jnp.where(pos == 7, 0, step) + y, NY)
            src = ((near * NX + xx) * NY + yy) * NC + core
        else:
            yy = (pos % 2) * 4 + xx
            src = (((1 - near) * NX + lax.rem(x + g - 4, NX)) * NY + yy) * NC + core
        hit = src * NCV + i == d
        both = jnp.concatenate([jnp.where(hit & (b == n), 1.0, 0.0).astype(BF) for n in range(BB)], axis=1)
        spread = jnp.dot(tm[...], both, preferred_element_type=F32).astype(BF)
        for n in range(BB):
            te[n, :, g * 128 : (g + 1) * 128] = spread[:, n * 128 : (n + 1) * 128]

    for k in (1, 3, 2):
        arrived(far_part(k), pf_recv.at[k])
        multiply(4 + k)

    terms = []
    for n in range(BB):
        acc = jnp.zeros((PAIRS, NA), F32)
        for c in range(NCV):
            acc += lax.dot_general(
                te[n, c * 128 : (c + 1) * 128, :], integ[c * NA : (c + 1) * NA, :],
                (((1,), (1,)), ((), ())), preferred_element_type=F32,
            )
        terms.append(acc)
    r0[...] = jnp.concatenate(terms, axis=1).reshape(8, NZH, NY, 128)

    for o in range(1, 8):
        other = lax.rem(idx_a + o, 8)
        put(r0.at[other], ra.at[o - 1], ra_send.at[o - 1], ra_recv.at[o - 1], h=other // NX, x=lax.rem(other, NX))
    part = r0[idx_a]
    for o in range(1, 8):
        arrived(ra.at[o - 1], ra_recv.at[o - 1])
    for o in range(1, 8):
        part += ra[o - 1]
    for q in range(16):
        rbs[q] = part[q // NY, q % NY : q % NY + 1, :]
    idx_b = zh * NY + y
    for o in (8, 12, 4, 7, 9, 11, 13, 5, 3, 6, 10, 14, 2, 15, 1):
        other = lax.rem(idx_b + o, 16)
        put(rbs.at[other], rb.at[o - 1], rb_send.at[o - 1], rb_recv.at[o - 1], zh=other // NY, y=lax.rem(other, NY))
    total = rbs[idx_b]
    for o in range(1, 16):
        arrived(rb.at[o - 1], rb_recv.at[o - 1])
    for o in range(1, 16):
        total += rb[o - 1]
    o_ref[...] = total

    @pl.when(zl == 0)
    def _():
        for o in range(15):
            left(piece, z_send.at[o])
    for o in range(NZL - 1):
        left(t_ref, t_send.at[o])
    for o in range(NX - 1):
        left(slab.at[7, x, h], xn_send.at[o])
        left(far_part(0), xf_send.at[o])
    for k in range(6):
        left(near_part(0), yr_send.at[k])
    for k in (6, 7):
        left(slab.at[4, 0:2, h], yr_send.at[k])
    for o in range(NY - 1):
        left(far, yf_send.at[o])
    for pos in range(8):
        left(near_part(pos), pn_send.at[pos])
    for k in range(4):
        left(far_part(k), pf_send.at[k])
    for o in range(7):
        left(r0.at[0], ra_send.at[o])
    for o in range(15):
        left(rbs.at[0], rb_send.at[o])


def body(factors, amplitudes):
    dma = pltpu.SemaphoreType.DMA
    row = pl.pallas_call(
        kernel,
        out_shape=jax.ShapeDtypeStruct((1, BB * NA), F32),
        in_specs=[pl.BlockSpec(memory_space=pltpu.VMEM)] * 2,
        out_specs=pl.BlockSpec(memory_space=pltpu.VMEM),
        scratch_shapes=[
            pltpu.VMEM((8, AUX), BF),
            pltpu.VMEM((16, 4, NC, 8, AUX), BF),
            pltpu.VMEM((NZL, NY, NC, NCV, V), BF),
            pltpu.VMEM((NCV * NA, AUX), BF),
            pltpu.VMEM((NCV * PAIRS, V), BF),
            pltpu.VMEM((BB, NCV * PAIRS, 1024), BF),
            pltpu.VMEM((NCV * NA, 1024), BF),
            pltpu.VMEM((8, NZH, NY, 128), F32),
            pltpu.VMEM((7, NZH, NY, 128), F32),
            pltpu.VMEM((16, 1, 128), F32),
            pltpu.VMEM((15, 1, 128), F32),
            dma((1,)), dma((15,)), dma((2,)), dma((7,)), dma((7,)), dma((3,)), dma((3,)), dma((8,)), dma((8,)),
            dma((7,)), dma((7,)), dma((3,)), dma((3,)), dma((8,)), dma((8,)), dma((4,)), dma((4,)),
            dma((7,)), dma((7,)), dma((15,)), dma((15,)),
        ],
        compiler_params=pltpu.CompilerParams(collective_id=0, has_side_effects=True),
    )(factors, amplitudes.reshape(NY, NC, NCV, V))
    return row.reshape(BB, 1, NA)


def solution(mesh):
    torus = Mesh(mesh.devices.reshape(NZH, NX, NY, NC, NZL), (ZH, X, Y, CORE, ZL))
    in_specs = (P(ZL, VIR, None), P(ZL, VIR, None))
    return jax.shard_map(body, mesh=torus, in_specs=in_specs, out_specs=P(None, VIR, ZL), check_vma=False)
```

time: 854 us -> 74.5 us (0.09)
  the two profiles are of different devices: /device:TPU:64 before, /device:TPU:128 now
where the time goes in v1:
time: 74.5 us; the launch traced here: 74.3 us
  Pallas kernels  72.3 us (97%)
  local copies, waits for them, and re-layouts  1.32 us (2%)
    pallas_call x1, Pallas kernels, body(): pl.pallas_call(kernel, out_shape=jax.ShapeDtypeStruct((1, BB * NA), F32),...  72.3 us

profile of v1, /device:TPU:128, one launch (start us, length us, event | category | flops | bytes accessed | tf_op | source)
XLA Modules:
  0.0 74.3 jit_solution(5886513329469919024)
XLA Ops:
  0.0 72.3 %shard_map.28 = f32[1,128]{1,0:T(1,128)} custom-call(bf16[64,4,1536]{2,1,0:T(4,128)(2,1)} %f_ref.1, bf16[8,2,4,512]{3,2,1,0:T(4,128)(2,1)} %bitcast.2), custom_call_target="tpu_custom_call" | custom-call | tf_op jit(solution)/shard_map/pallas_call | solution.py:262
  72.3 0.0 copy-start
  72.3 0.5 broadcast.3
  72.9 0.2 copy-done
  73.0 0.7 reduce.3
  73.7 0.6 reshape.7
Async XLA Ops:
  72.3 0.7 copy-start

commit v2 on v1

v2 whole, which is shorter than its diff:
```python
import jax
import jax.numpy as jnp
from jax import lax
from jax.experimental import pallas as pl
from jax.experimental.pallas import tpu as pltpu
from jax.sharding import Mesh
from jax.sharding import PartitionSpec as P

ZH, X, Y, CORE, ZL = "vir_0", "vir_1", "vir_2", "vir_3", "out"
VIR = (ZH, X, Y, CORE)
NZH, NX, NY, NC, NZL = 2, 4, 8, 2, 8
BB, NCV, NA, AUX, V, PAIRS = 2, 4, 64, 1536, 512, 128
MESH = pl.DeviceIdType.MESH
BF, F32 = jnp.bfloat16, jnp.float32


def kernel(
    f_ref, t_ref, o_ref,
    piece, slab, traw, fm, tm, pick, te, integ, r0, ra, rbs, rb,
    local_sem, mid_sem, z_send, z_recv, t_send, t_recv, xn_send, xn_recv, yr_send, yr_recv,
    yf_send, yf_recv, xf_send, xf_recv, pn_send, pn_recv, pf_send, pf_recv,
    ra_send, ra_recv, rb_send, rb_recv,
):
    zh, x, y, h, zl = (lax.axis_index(n) for n in (ZH, X, Y, CORE, ZL))
    near = jnp.where(zl <= NZL // 2, zh, 1 - zh)
    names = {"zh": ZH, "x": X, "y": Y, "h": CORE, "zl": ZL}

    def to(where):
        return dict(device_id={names[k]: v for k, v in where.items()}, device_id_type=MESH)

    def put(src, dst, ssem, rsem, **where):
        pltpu.make_async_remote_copy(src_ref=src, dst_ref=dst, send_sem=ssem, recv_sem=rsem, **to(where)).start()

    def arrived(dst, rsem):
        pltpu.make_async_copy(dst, dst, rsem).wait()

    left = arrived

    barrier = pltpu.get_barrier_semaphore()
    idx_z = zh * NZL + zl
    idx_a = h * NX + x
    idx_b = zh * NY + y

    def at_z(o):
        other = lax.rem(idx_z + o + 16, 16)
        return dict(zh=other // NZL, zl=lax.rem(other, NZL))

    def at_a(o):
        other = lax.rem(idx_a + o, 8)
        return other, dict(h=other // NX, x=lax.rem(other, NX))

    for o in (-4, 4, -3, 3, -2, 2, -1, 1):
        pl.semaphore_signal(barrier, inc=1, **to(at_z(o)))
    for o in range(1, 8):
        pl.semaphore_signal(barrier, inc=1, **to(at_a(o)[1]))
    for o in range(1, NY):
        pl.semaphore_signal(barrier, inc=1, **to(dict(y=lax.rem(y + o, NY))))

    piece[0:4, :] = f_ref[0]
    piece[4:8, :] = f_ref[1]
    own_t = pltpu.make_async_copy(t_ref, traw.at[zl], local_sem.at[0])
    own_t.start()
    for c in range(NCV):
        fm[c * NA : (c + 1) * NA, :] = f_ref[:, c, :]

    pl.semaphore_wait(barrier, 8 + 7 + 7)
    pl.semaphore_signal(mid_sem, inc=1, **to(at_z(-4)))

    near_own, far_own = slab.at[7, x, h], slab.at[8, 2, h]

    @pl.when(zl == 0)
    def _():
        own = pltpu.make_async_copy(piece, near_own, local_sem.at[1])
        own.start()
        put(piece, near_own, z_send.at[0], z_recv.at[0], **at_z(4))
        put(piece, far_own, z_send.at[1], z_recv.at[1], **at_z(-4))
        for s, o in enumerate((3, -3, 2, -2, 1, -1)):
            put(piece, near_own, z_send.at[2 + s], z_recv.at[0], **at_z(o))
        own.wait()

    @pl.when(zl != 0)
    def _():
        arrived(near_own, z_recv.at[0])

    @pl.when(zl == 4)
    def _():
        for s, o in enumerate((4, 3, 2, 1)):
            put(near_own, far_own, z_send.at[s], z_recv.at[1], **at_z(o))

    for o in range(1, NX):
        put(near_own, near_own, xn_send.at[o - 1], xn_recv.at[o - 1], x=lax.rem(x + o, NX))

    mate = lax.rem(zl + 4, NZL)
    quad = [(zl // 4) * 4 + lax.rem(zl + o, 4) for o in range(1, 4)]

    def amplitudes_out():
        put(t_ref, traw.at[zl], t_send.at[0], t_recv.at[0], zl=mate)
        for o in range(3):
            put(t_ref, traw.at[zl], t_send.at[1 + o], t_recv.at[1 + o], zl=quad[o])

    def amplitudes_on():
        arrived(t_ref, t_recv.at[0])
        for o in range(3):
            put(traw.at[mate], traw.at[mate], t_send.at[4 + o], t_recv.at[4 + o], zl=quad[o])

    up, down = lax.rem(y + 1, NY), lax.rem(y + NY - 1, NY)
    xup, xdown = lax.rem(x + 1, NX), lax.rem(x + NX - 1, NX)

    def near_part(pos):
        return slab.at[pos, :, h]

    def near_half(pos, f):
        return slab.at[pos, 2 * f : 2 * f + 2, h]

    def ring(src, dst, f, y_to):
        s = 2 * dst + f
        put(near_half(src, f), near_half(dst, f), yr_send.at[s], yr_recv.at[s], y=y_to)

    def ring_arrived(pos, f):
        arrived(near_half(pos, f), yr_recv.at[2 * pos + f])

    def share_near(pos):
        put(near_part(pos), near_part(pos), pn_send.at[pos], pn_recv.at[pos], h=1 - h)

    def near_shared(pos):
        arrived(near_part(pos), pn_recv.at[pos])

    def far_half(k, c):
        return slab.at[8 + 2 * k + c, :, h]

    def far_on(src, dst, c, x_to):
        s = 2 * dst + c - 2
        put(far_half(src, c), far_half(dst, c), xf_send.at[s], xf_recv.at[s], x=x_to)

    def far_arrived(k, c):
        arrived(far_half(k, c), xf_recv.at[2 * k + c - 2])

    def share_far(k, c):
        s = 2 * k + c
        put(far_half(k, c), far_half(k, c), pf_send.at[s], pf_recv.at[s], h=1 - h)

    def far_shared(k):
        for c in range(2):
            arrived(far_half(k, c), pf_recv.at[2 * k + c])

    def multiply(g):
        rows = slab[2 * g : 2 * g + 2].reshape(128, AUX)
        tile = lax.dot_general(fm[...], rows, (((1,), (1,)), ((), ())), preferred_element_type=F32)
        integ[:, g * 128 : (g + 1) * 128] = tile.astype(BF)

    amplitudes_out()
    for o in range(1, NX):
        arrived(near_own, xn_recv.at[o - 1])
    for f in range(2):
        ring(7, 0, f, up)
        ring(7, 1, f, down)
    share_near(7)

    arrived(far_own, z_recv.at[1])

    @pl.when(zl == 4)
    def _():
        for s, o in enumerate((-3, -2, -1)):
            put(far_own, far_own, z_send.at[4 + s], z_recv.at[1], **at_z(o))

    pl.semaphore_wait(mid_sem, 1)
    for o in (7, 1, 2, 6, 3, 5, 4):
        q = (2 - o) % NY
        put(far_own, slab.at[8 + q // 4, q % 4, h], yf_send.at[o - 1], yf_recv.at[o - 1], y=lax.rem(y + o, NY))

    for step in range(2):
        for f in range(2):
            ring_arrived(2 * step, f)
            ring(2 * step, 2 * step + 2, f, up)
            ring_arrived(2 * step + 1, f)
            ring(2 * step + 1, 2 * step + 3, f, down)
        share_near(2 * step)
        share_near(2 * step + 1)
        for o in ((1, 2, 7), (3, 4, 5, 6))[step]:
            arrived(far_own, yf_recv.at[o - 1])
        far_on(0, 3, step, xup)
        far_on(0, 1, step, xdown)
        share_far(0, step)

    d = lax.broadcasted_iota(jnp.int32, (V, 128), 0)
    for g in range(8):
        j = lax.broadcasted_iota(jnp.int32, (1, 128), 1) + g * 128
        pos, xx, core, b, i = j // 64, (j // 16) % 4, (j // 8) % 2, (j // 4) % 2, j % 4
        if g < 4:
            step = jnp.where(pos % 2 == 0, NY - 1 - pos // 2, pos // 2 + 1)
            yy = lax.rem(jnp.where(pos == 7, 0, step) + y, NY)
            src = ((near * NX + xx) * NY + yy) * NC + core
        else:
            yy = lax.rem((pos % 2) * 4 + xx + y + NY - 2, NY)
            src = (((1 - near) * NX + lax.rem(x + g - 4, NX)) * NY + yy) * NC + core
        for n in range(BB):
            want = jnp.where(b == n, src * NCV + i, -1)
            pick[g, :, n * 128 : (n + 1) * 128] = jnp.where(d == want, 1.0, 0.0).astype(BF)

    amplitudes_on()
    near_shared(0)
    near_shared(1)
    multiply(0)

    ring_arrived(4, 0)
    ring(4, 6, 0, up)
    ring_arrived(5, 1)
    ring(5, 6, 1, down)
    ring_arrived(4, 1)
    ring_arrived(5, 0)
    share_near(4)
    share_near(5)
    far_arrived(3, 0)
    far_on(3, 2, 0, xup)
    share_far(3, 0)
    far_arrived(1, 0)
    share_far(1, 0)
    near_shared(2)
    near_shared(3)
    multiply(1)
    far_arrived(1, 1)
    far_on(1, 2, 1, xdown)
    share_far(1, 1)
    far_arrived(3, 1)
    share_far(3, 1)
    near_shared(4)
    near_shared(5)
    multiply(2)
    ring_arrived(6, 0)
    ring_arrived(6, 1)
    share_near(6)
    far_shared(0)
    multiply(4)
    for c in range(2):
        far_arrived(2, c)
        share_far(2, c)

    own_t.wait()
    for o in range(1, NZL - 1):
        arrived(t_ref, t_recv.at[o])
    for s in range(NZL):
        szh, sx = s // NX, s % NX
        for core in range(NC):
            for c in range(NCV):
                row = c * 128 + core * 64 + sx * 16 + szh * 8
                tm[row : row + 8, :] = traw[s, :, core, c, :]
    for g in range(8):
        spread = jnp.dot(tm[...], pick[g], preferred_element_type=F32).astype(BF)
        for n in range(BB):
            te[n, :, g * 128 : (g + 1) * 128] = spread[:, n * 128 : (n + 1) * 128]

    near_shared(6)
    near_shared(7)
    multiply(3)
    for k in (1, 3, 2):
        far_shared(k)
        multiply(4 + k)

    terms = []
    for n in range(BB):
        acc = jnp.zeros((PAIRS, NA), F32)
        for c in range(NCV):
            acc += lax.dot_general(
                te[n, c * 128 : (c + 1) * 128, :], integ[c * NA : (c + 1) * NA, :],
                (((1,), (1,)), ((), ())), preferred_element_type=F32,
            )
        terms.append(acc)
    r0[...] = jnp.concatenate(terms, axis=1).reshape(8, NZH, NY, 128)

    for o in range(1, 8):
        other, where = at_a(o)
        put(r0.at[other], ra.at[o - 1], ra_send.at[o - 1], ra_recv.at[o - 1], **where)
    part = r0[idx_a]
    for o in range(1, 8):
        arrived(ra.at[o - 1], ra_recv.at[o - 1])
    for o in range(1, 8):
        part += ra[o - 1]
    for q in range(16):
        rbs[q] = part[q // NY, q % NY : q % NY + 1, :]
    for o in (8, 12, 4, 7, 9, 11, 13, 5, 3, 6, 10, 14, 2, 15, 1):
        other = lax.rem(idx_b + o, 16)
        put(rbs.at[other], rb.at[o - 1], rb_send.at[o - 1], rb_recv.at[o - 1], zh=other // NY, y=lax.rem(other, NY))
    total = rbs[idx_b]
    for o in range(1, 16):
        arrived(rb.at[o - 1], rb_recv.at[o - 1])
    for o in range(1, 16):
        total += rb[o - 1]
    for n in range(BB):
        o_ref[n] = total[:, n * NA : (n + 1) * NA]

    @pl.when(zl == 0)
    def _():
        for s in range(8):
            left(piece, z_send.at[s])

    @pl.when(zl == 4)
    def _():
        for s in range(7):
            left(far_own, z_send.at[s])

    for o in range(NZL - 1):
        left(t_ref, t_send.at[o])
    for o in range(NX - 1):
        left(near_own, xn_send.at[o])
    for s in range(14):
        left(near_half(0, 0), yr_send.at[s])
    for o in range(NY - 1):
        left(far_own, yf_send.at[o])
    for s in range(6):
        left(far_half(0, 0), xf_send.at[s])
    for s in range(8):
        left(near_part(0), pn_send.at[s])
        left(far_half(0, 0), pf_send.at[s])
    for o in range(7):
        left(r0.at[0], ra_send.at[o])
    for o in range(15):
        left(rbs.at[0], rb_send.at[o])


def body(factors, amplitudes):
    dma = pltpu.SemaphoreType.DMA
    return pl.pallas_call(
        kernel,
        out_shape=jax.ShapeDtypeStruct((BB, 1, NA), F32),
        in_specs=[pl.BlockSpec(memory_space=pltpu.VMEM)] * 2,
        out_specs=pl.BlockSpec(memory_space=pltpu.VMEM),
        scratch_shapes=[
            pltpu.VMEM((8, AUX), BF),
            pltpu.VMEM((16, 4, NC, 8, AUX), BF),
            pltpu.VMEM((NZL, NY, NC, NCV, V), BF),
            pltpu.VMEM((NCV * NA, AUX), BF),
            pltpu.VMEM((NCV * PAIRS, V), BF),
            pltpu.VMEM((8, V, BB * 128), BF),
            pltpu.VMEM((BB, NCV * PAIRS, 1024), BF),
            pltpu.VMEM((NCV * NA, 1024), BF),
            pltpu.VMEM((8, NZH, NY, 128), F32),
            pltpu.VMEM((7, NZH, NY, 128), F32),
            pltpu.VMEM((16, 1, 128), F32),
            pltpu.VMEM((15, 1, 128), F32),
            dma((2,)), pltpu.SemaphoreType.REGULAR, dma((8,)), dma((2,)), dma((7,)), dma((7,)), dma((3,)), dma((3,)), dma((14,)), dma((14,)), dma((7,)),
            dma((7,)), dma((6,)), dma((6,)), dma((8,)), dma((8,)), dma((8,)), dma((8,)), dma((7,)), dma((7,)), dma((15,)), dma((15,)),
        ],
        compiler_params=pltpu.CompilerParams(collective_id=0, has_side_effects=True),
    )(factors, amplitudes.reshape(NY, NC, NCV, V))


def solution(mesh):
    torus = Mesh(mesh.devices.reshape(NZH, NX, NY, NC, NZL), (ZH, X, Y, CORE, ZL))
    in_specs = (P(ZL, VIR, None), P(ZL, VIR, None))
    return jax.shard_map(body, mesh=torus, in_specs=in_specs, out_specs=P(None, VIR, ZL), check_vma=False)
```

time: 74.5 us -> 71.1 us (0.954)
  the two profiles are of different devices: /device:TPU:128 before, /device:TPU:64 now
where the time goes in v2:
time: 71.1 us; the launch traced here: 71 us
  Pallas kernels  69.7 us (98%)
  local copies, waits for them, and re-layouts  1.24 us (2%)
    pallas_call x1, Pallas kernels, body(): pl.pallas_call(kernel, out_shape=jax.ShapeDtypeStruct((BB, 1, NA), F32),...  69.7 us

profile of v2, /device:TPU:64, one launch (start us, length us, event | category | flops | bytes accessed | tf_op | source)
XLA Modules:
  0.0 71.0 jit_solution(12874498242533941500)
XLA Ops:
  0.0 69.7 %shard_map.28 = f32[2,1,64]{2,1,0:T(1,128)} custom-call(bf16[64,4,1536]{2,1,0:T(4,128)(2,1)} %f_ref.1, bf16[8,2,4,512]{3,2,1,0:T(4,128)(2,1)} %bitcast.1), custom_call_target="tpu_custom_call" | custom-call | tf_op jit(solution)/shard_map/pallas_call | solution.py:322
  69.7 1.2 %copy.4 = f32[2,1,64]{2,1,0:T(1,128)} copy(f32[2,1,64]{2,1,0:T(1,128)} %shard_map.28) | data formatting | bytes 1024

commit v3 on v2

v3 whole, which is shorter than its diff:
```python
import jax
import jax.numpy as jnp
from jax import lax
from jax.experimental import pallas as pl
from jax.experimental.pallas import tpu as pltpu
from jax.sharding import Mesh
from jax.sharding import PartitionSpec as P

ZH, X, Y, CORE, ZL = "vir_0", "vir_1", "vir_2", "vir_3", "out"
VIR = (ZH, X, Y, CORE)
NZH, NX, NY, NC, NZL = 2, 4, 8, 2, 8
BB, NCV, NA, AUX, V, PAIRS = 2, 4, 64, 1536, 512, 128
MESH = pl.DeviceIdType.MESH
BF, F32 = jnp.bfloat16, jnp.float32


def kernel(
    f_ref, t_ref, o_ref,
    piece, slab, traw, fm, tm, pick, te, integ, r0, ra, rbs, rb,
    local_sem, mid_sem, z_send, z_recv, t_send, t_recv, xn_send, xn_recv, yr_send, yr_recv,
    yf_send, yf_recv, xf_send, xf_recv, pn_send, pn_recv, pf_send, pf_recv,
    ra_send, ra_recv, rb_send, rb_recv,
):
    zh, x, y, h, zl = (lax.axis_index(n) for n in (ZH, X, Y, CORE, ZL))
    near = jnp.where(zl <= NZL // 2, zh, 1 - zh)
    names = {"zh": ZH, "x": X, "y": Y, "h": CORE, "zl": ZL}

    def to(where):
        return dict(device_id={names[k]: v for k, v in where.items()}, device_id_type=MESH)

    def put(src, dst, ssem, rsem, **where):
        pltpu.make_async_remote_copy(src_ref=src, dst_ref=dst, send_sem=ssem, recv_sem=rsem, **to(where)).start()

    def arrived(dst, rsem):
        pltpu.make_async_copy(dst, dst, rsem).wait()

    left = arrived

    barrier = pltpu.get_barrier_semaphore()
    idx_z = zh * NZL + zl
    idx_a = h * NX + x
    idx_b = zh * NY + y

    def at_z(o):
        other = lax.rem(idx_z + o + 16, 16)
        return dict(zh=other // NZL, zl=lax.rem(other, NZL))

    def at_a(o):
        other = lax.rem(idx_a + o, 8)
        return other, dict(h=other // NX, x=lax.rem(other, NX))

    for o in (-4, 4, -3, 3, -2, 2, -1, 1):
        pl.semaphore_signal(barrier, inc=1, **to(at_z(o)))
    for o in range(1, 8):
        pl.semaphore_signal(barrier, inc=1, **to(at_a(o)[1]))
    for o in range(1, NY):
        pl.semaphore_signal(barrier, inc=1, **to(dict(y=lax.rem(y + o, NY))))

    piece[0:4, :] = f_ref[0]
    piece[4:8, :] = f_ref[1]
    own_t = pltpu.make_async_copy(t_ref, traw.at[zl], local_sem.at[0])
    own_t.start()

    pl.semaphore_wait(barrier, 8 + 7 + 7)
    pl.semaphore_signal(mid_sem, inc=1, **to(at_z(-4)))

    near_own, far_own = slab.at[7, x, h], slab.at[8, 2, h]

    @pl.when(zl == 0)
    def _():
        own = pltpu.make_async_copy(piece, near_own, local_sem.at[1])
        own.start()
        put(piece, near_own, z_send.at[0], z_recv.at[0], **at_z(4))
        put(piece, far_own, z_send.at[1], z_recv.at[1], **at_z(-4))
        for s, o in enumerate((3, -3, 2, -2, 1, -1)):
            put(piece, near_own, z_send.at[2 + s], z_recv.at[0], **at_z(o))
        own.wait()

    for c in range(NCV):
        fm[c * NA : (c + 1) * NA, :] = f_ref[:, c, :]
    d = lax.broadcasted_iota(jnp.int32, (V, 128), 0)
    for g in range(8):
        j = lax.broadcasted_iota(jnp.int32, (1, 128), 1) + g * 128
        pos, xx, core, b, i = j // 64, (j // 16) % 4, (j // 8) % 2, (j // 4) % 2, j % 4
        if g < 4:
            step = jnp.where(pos % 2 == 0, NY - 1 - pos // 2, pos // 2 + 1)
            yy = lax.rem(jnp.where(pos == 7, 0, step) + y, NY)
            src = ((near * NX + xx) * NY + yy) * NC + core
        else:
            yy = lax.rem((pos % 2) * 4 + xx + y + NY - 2, NY)
            src = (((1 - near) * NX + lax.rem(x + g - 4, NX)) * NY + yy) * NC + core
        for n in range(BB):
            want = jnp.where(b == n, src * NCV + i, -1)
            pick[g, :, n * 128 : (n + 1) * 128] = jnp.where(d == want, 1.0, 0.0).astype(BF)

    @pl.when(zl != 0)
    def _():
        arrived(near_own, z_recv.at[0])

    @pl.when(zl == 4)
    def _():
        for s, o in enumerate((4, 3, 2, 1)):
            put(near_own, far_own, z_send.at[s], z_recv.at[1], **at_z(o))

    for o in range(1, NX):
        put(near_own, near_own, xn_send.at[o - 1], xn_recv.at[o - 1], x=lax.rem(x + o, NX))

    mate = lax.rem(zl + 4, NZL)
    quad = [(zl // 4) * 4 + lax.rem(zl + o, 4) for o in range(1, 4)]

    def amplitudes_out():
        put(t_ref, traw.at[zl], t_send.at[0], t_recv.at[0], zl=mate)
        for o in range(3):
            put(t_ref, traw.at[zl], t_send.at[1 + o], t_recv.at[1 + o], zl=quad[o])

    def amplitudes_on():
        arrived(t_ref, t_recv.at[0])
        for o in range(3):
            put(traw.at[mate], traw.at[mate], t_send.at[4 + o], t_recv.at[4 + o], zl=quad[o])

    up, down = lax.rem(y + 1, NY), lax.rem(y + NY - 1, NY)
    xup, xdown = lax.rem(x + 1, NX), lax.rem(x + NX - 1, NX)

    def near_part(pos):
        return slab.at[pos, :, h]

    def near_half(pos, f):
        return slab.at[pos, 2 * f : 2 * f + 2, h]

    def ring(src, dst, f, y_to):
        s = 2 * dst + f
        put(near_half(src, f), near_half(dst, f), yr_send.at[s], yr_recv.at[s], y=y_to)

    def ring_arrived(pos, f):
        arrived(near_half(pos, f), yr_recv.at[2 * pos + f])

    def share_near(pos):
        put(near_part(pos), near_part(pos), pn_send.at[pos], pn_recv.at[pos], h=1 - h)

    def near_shared(pos):
        arrived(near_part(pos), pn_recv.at[pos])

    def far_chunk(k, m):
        first = (2, 0, 0, 2)[m]
        return slab.at[8 + 2 * k + m // 2, first : first + 2, h]

    def far_on(src, dst, m, x_to):
        s = 4 * (dst - 1) + m
        put(far_chunk(src, m), far_chunk(dst, m), xf_send.at[s], xf_recv.at[s], x=x_to)

    def far_arrived(k, m):
        arrived(far_chunk(k, m), xf_recv.at[4 * (k - 1) + m])

    def share_far(k, m):
        s = 4 * k + m
        put(far_chunk(k, m), far_chunk(k, m), pf_send.at[s], pf_recv.at[s], h=1 - h)

    def far_shared(k):
        for m in range(4):
            arrived(far_chunk(k, m), pf_recv.at[4 * k + m])

    def multiply(g):
        rows = slab[2 * g : 2 * g + 2].reshape(128, AUX)
        tile = lax.dot_general(fm[...], rows, (((1,), (1,)), ((), ())), preferred_element_type=F32)
        integ[:, g * 128 : (g + 1) * 128] = tile.astype(BF)

    amplitudes_out()
    for o in range(1, NX):
        arrived(near_own, xn_recv.at[o - 1])
    for f in range(2):
        ring(7, 0, f, up)
        ring(7, 1, f, down)
    share_near(7)

    arrived(far_own, z_recv.at[1])

    @pl.when(zl == 4)
    def _():
        for s, o in enumerate((-3, -2, -1)):
            put(far_own, far_own, z_send.at[4 + s], z_recv.at[1], **at_z(o))

    pl.semaphore_wait(mid_sem, 1)

    def far_place(o):
        q = (2 - o) % NY
        return slab.at[8 + q // 4, q % 4, h]

    for o in (4, 7, 1, 3, 2, 6, 5):
        put(far_own, far_place(o), yf_send.at[o - 1], yf_recv.at[o - 1], y=lax.rem(y + o, NY))

    def ring_on(step):
        for f in range(2):
            ring_arrived(2 * step, f)
            ring(2 * step, 2 * step + 2, f, up)
            ring_arrived(2 * step + 1, f)
            ring(2 * step + 1, 2 * step + 3, f, down)
        share_near(2 * step)
        share_near(2 * step + 1)

    def column_on(m, *offsets):
        for o in offsets:
            arrived(far_own, yf_recv.at[o - 1])
        if m == 3:
            far_on(0, 2, m, lax.rem(x + 2, NX))
        far_on(0, 3, m, xup)
        far_on(0, 1, m, xdown)
        share_far(0, m)

    def rows_on(m):
        first, second, x_to = (3, 1, xup) if m % 2 == 0 else (1, 3, xdown)
        far_arrived(first, m)
        if m < 3:
            far_on(first, 2, m, x_to)
        share_far(first, m)
        far_arrived(second, m)
        share_far(second, m)

    def gather_pairs(half):
        for sx in range(NX):
            for core in range(NC):
                for c in range(NCV):
                    row = c * 64 + core * 32 + sx * 8
                    tm[row : row + 8, :] = traw[half * NX + sx, :, core, c, :]

    def expand(half, groups):
        for g in groups:
            spread = jnp.dot(tm[...], pick[g], preferred_element_type=F32).astype(BF)
            for c in range(NCV):
                for n in range(BB):
                    te[c, half, n, :, g * 128 : (g + 1) * 128] = spread[c * 64 : (c + 1) * 64, n * 128 : (n + 1) * 128]

    ring_on(0)
    column_on(0, 7)
    column_on(1, 1, 2)
    amplitudes_on()
    own_t.wait()
    for o in range(1, 4):
        arrived(t_ref, t_recv.at[o])
    gather_pairs(zl // 4)
    expand(zl // 4, range(4))
    ring_on(1)
    column_on(2, 6, 5)
    expand(zl // 4, range(4, 8))
    rows_on(0)
    column_on(3, 3, 4)
    near_shared(0)
    near_shared(1)
    multiply(0)
    rows_on(1)
    ring_arrived(4, 0)
    ring(4, 6, 0, up)
    ring_arrived(5, 1)
    ring(5, 6, 1, down)
    far_shared(0)
    multiply(4)
    rows_on(2)
    ring_arrived(4, 1)
    ring_arrived(5, 0)
    share_near(4)
    share_near(5)
    near_shared(2)
    near_shared(3)
    multiply(1)
    rows_on(3)
    for o in range(4, NZL - 1):
        arrived(t_ref, t_recv.at[o])
    gather_pairs(1 - zl // 4)
    expand(1 - zl // 4, range(4))
    for m in range(2):
        far_arrived(2, m)
        share_far(2, m)
    ring_arrived(6, 0)
    ring_arrived(6, 1)
    share_near(6)
    expand(1 - zl // 4, range(4, 8))
    for m in range(2, 4):
        far_arrived(2, m)
        share_far(2, m)
    near_shared(4)
    near_shared(5)
    multiply(2)
    for k in (1, 3):
        far_shared(k)
        multiply(4 + k)

    def terms(lo, hi):
        return sum(
            lax.dot_general(
                te[c, :, :, :, lo:hi].reshape(BB * PAIRS, hi - lo), integ[c * NA : (c + 1) * NA, lo:hi],
                (((1,), (1,)), ((), ())), preferred_element_type=F32,
            )
            for c in range(NCV)
        )

    acc = terms(0, 384) + terms(512, 768) + terms(896, 1024)
    near_shared(6)
    near_shared(7)
    multiply(3)
    far_shared(2)
    multiply(6)
    acc = (acc + terms(384, 512) + terms(768, 896)).reshape(NZH, BB, 8, NY, NA)
    for z in range(NZH):
        r0[:, z] = jnp.concatenate([acc[z, n] for n in range(BB)], axis=-1)

    for o in range(1, 8):
        other, where = at_a(o)
        put(r0.at[other], ra.at[o - 1], ra_send.at[o - 1], ra_recv.at[o - 1], **where)
    part = r0[idx_a]
    for o in range(1, 8):
        arrived(ra.at[o - 1], ra_recv.at[o - 1])
    for o in range(1, 8):
        part += ra[o - 1]
    for q in range(16):
        rbs[q] = part[q // NY, q % NY : q % NY + 1, :]
    for o in (8, 12, 4, 7, 9, 11, 13, 5, 3, 6, 10, 14, 2, 15, 1):
        other = lax.rem(idx_b + o, 16)
        put(rbs.at[other], rb.at[o - 1], rb_send.at[o - 1], rb_recv.at[o - 1], zh=other // NY, y=lax.rem(other, NY))
    total = rbs[idx_b]
    for o in range(1, 16):
        arrived(rb.at[o - 1], rb_recv.at[o - 1])
    for o in range(1, 16):
        total += rb[o - 1]
    for n in range(BB):
        o_ref[n] = total[:, n * NA : (n + 1) * NA]

    @pl.when(zl == 0)
    def _():
        for s in range(8):
            left(piece, z_send.at[s])

    @pl.when(zl == 4)
    def _():
        for s in range(7):
            left(far_own, z_send.at[s])

    for o in range(NZL - 1):
        left(t_ref, t_send.at[o])
    for o in range(NX - 1):
        left(near_own, xn_send.at[o])
    for s in range(14):
        left(near_half(0, 0), yr_send.at[s])
    for o in range(NY - 1):
        left(far_own, yf_send.at[o])
    for s in range(12):
        left(far_chunk(0, 0), xf_send.at[s])
    for s in range(8):
        left(near_part(0), pn_send.at[s])
    for s in range(16):
        left(far_chunk(0, 0), pf_send.at[s])
    for o in range(7):
        left(r0.at[0], ra_send.at[o])
    for o in range(15):
        left(rbs.at[0], rb_send.at[o])


def body(factors, amplitudes):
    dma = pltpu.SemaphoreType.DMA
    return pl.pallas_call(
        kernel,
        out_shape=jax.ShapeDtypeStruct((BB, 1, NA), F32),
        in_specs=[pl.BlockSpec(memory_space=pltpu.VMEM)] * 2,
        out_specs=pl.BlockSpec(memory_space=pltpu.VMEM),
        scratch_shapes=[
            pltpu.VMEM((8, AUX), BF),
            pltpu.VMEM((16, 4, NC, 8, AUX), BF),
            pltpu.VMEM((NZL, NY, NC, NCV, V), BF),
            pltpu.VMEM((NCV * NA, AUX), BF),
            pltpu.VMEM((NCV * 64, V), BF),
            pltpu.VMEM((8, V, BB * 128), BF),
            pltpu.VMEM((NCV, NZH, BB, 64, 1024), BF),
            pltpu.VMEM((NCV * NA, 1024), BF),
            pltpu.VMEM((8, NZH, NY, 128), F32),
            pltpu.VMEM((7, NZH, NY, 128), F32),
            pltpu.VMEM((16, 1, 128), F32),
            pltpu.VMEM((15, 1, 128), F32),
            dma((2,)), pltpu.SemaphoreType.REGULAR, dma((8,)), dma((2,)), dma((7,)), dma((7,)), dma((3,)), dma((3,)), dma((14,)), dma((14,)), dma((7,)),
            dma((7,)), dma((12,)), dma((12,)), dma((8,)), dma((8,)), dma((16,)), dma((16,)), dma((7,)), dma((7,)), dma((15,)), dma((15,)),
        ],
        compiler_params=pltpu.CompilerParams(collective_id=0, has_side_effects=True),
    )(factors, amplitudes.reshape(NY, NC, NCV, V))


def solution(mesh):
    torus = Mesh(mesh.devices.reshape(NZH, NX, NY, NC, NZL), (ZH, X, Y, CORE, ZL))
    in_specs = (P(ZL, VIR, None), P(ZL, VIR, None))
    return jax.shard_map(body, mesh=torus, in_specs=in_specs, out_specs=P(None, VIR, ZL), check_vma=False)
```

time: 71.1 us -> 68.4 us (0.962)
  Pallas kernels: 69.7 us -> 66.9 us
    pallas_call x1, Pallas kernels: 69.7 us -> 66.9 us  [body(): pl.pallas_call(kernel, out_shape=jax.ShapeDtypeStruct((BB, 1, NA), F32),...]
where the time goes in v3:
time: 68.4 us; the launch traced here: 68.2 us
  Pallas kernels  66.9 us (98%)
  local copies, waits for them, and re-layouts  1.24 us (2%)
    pallas_call x1, Pallas kernels, body(): pl.pallas_call(kernel, out_shape=jax.ShapeDtypeStruct((BB, 1, NA), F32),...  66.9 us

profile of v3, /device:TPU:64, one launch (start us, length us, event | category | flops | bytes accessed | tf_op | source)
XLA Modules:
  0.0 68.2 jit_solution(3831590146921040499)
XLA Ops:
  0.0 66.9 %shard_map.28 = f32[2,1,64]{2,1,0:T(1,128)} custom-call(bf16[64,4,1536]{2,1,0:T(4,128)(2,1)} %f_ref.1, bf16[8,2,4,512]{3,2,1,0:T(4,128)(2,1)} %bitcast.1), custom_call_target="tpu_custom_call" | custom-call | tf_op jit(solution)/shard_map/pallas_call | solution.py:358
  66.9 1.2 %copy.4 = f32[2,1,64]{2,1,0:T(1,128)} copy(f32[2,1,64]{2,1,0:T(1,128)} %shard_map.28) | data formatting | bytes 1024

commit v4 on v3

--- a/solution.py
+++ b/solution.py
@@ -15,8 +15,8 @@
 
 
 def kernel(
-    f_ref, t_ref, o_ref,
-    piece, slab, traw, fm, tm, pick, te, integ, r0, ra, rbs, rb,
+    f_hbm, t_hbm, o_ref,
+    f_ref, piece, slab, traw, fm, tm, pick, te, integ, r0, ra, rbs, rb,
     local_sem, mid_sem, z_send, z_recv, t_send, t_recv, xn_send, xn_recv, yr_send, yr_recv,
     yf_send, yf_recv, xf_send, xf_recv, pn_send, pn_recv, pf_send, pf_recv,
     ra_send, ra_recv, rb_send, rb_recv,
@@ -56,10 +56,15 @@
     for o in range(1, NY):
         pl.semaphore_signal(barrier, inc=1, **to(dict(y=lax.rem(y + o, NY))))
 
+    own_f = pltpu.make_async_copy(f_hbm, f_ref, local_sem.at[2])
+    own_f.start()
+    t_ref = traw.at[zl]
+    own_t = pltpu.make_async_copy(t_hbm, t_ref, local_sem.at[0])
+    own_t.start()
+    own_f.wait()
     piece[0:4, :] = f_ref[0]
     piece[4:8, :] = f_ref[1]
-    own_t = pltpu.make_async_copy(t_ref, traw.at[zl], local_sem.at[0])
-    own_t.start()
+    own_t.wait()
 
     pl.semaphore_wait(barrier, 8 + 7 + 7)
     pl.semaphore_signal(mid_sem, inc=1, **to(at_z(-4)))
@@ -200,7 +205,7 @@
     def column_on(m, *offsets):
         for o in offsets:
             arrived(far_own, yf_recv.at[o - 1])
-        if m == 3:
+        if m >= 2:
             far_on(0, 2, m, lax.rem(x + 2, NX))
         far_on(0, 3, m, xup)
         far_on(0, 1, m, xdown)
@@ -209,7 +214,7 @@
     def rows_on(m):
         first, second, x_to = (3, 1, xup) if m % 2 == 0 else (1, 3, xdown)
         far_arrived(first, m)
-        if m < 3:
+        if m < 2:
             far_on(first, 2, m, x_to)
         share_far(first, m)
         far_arrived(second, m)
@@ -233,7 +238,6 @@
     column_on(0, 7)
     column_on(1, 1, 2)
     amplitudes_on()
-    own_t.wait()
     for o in range(1, 4):
         arrived(t_ref, t_recv.at[o])
     gather_pairs(zl // 4)
@@ -312,17 +316,9 @@
         part += ra[o - 1]
     for q in range(16):
         rbs[q] = part[q // NY, q % NY : q % NY + 1, :]
-    for o in (8, 12, 4, 7, 9, 11, 13, 5, 3, 6, 10, 14, 2, 15, 1):
+    for o in (12, 11, 13, 10, 14, 9, 15, 8, 4, 5, 3, 6, 2, 7, 1):
         other = lax.rem(idx_b + o, 16)
         put(rbs.at[other], rb.at[o - 1], rb_send.at[o - 1], rb_recv.at[o - 1], zh=other // NY, y=lax.rem(other, NY))
-    total = rbs[idx_b]
-    for o in range(1, 16):
-        arrived(rb.at[o - 1], rb_recv.at[o - 1])
-    for o in range(1, 16):
-        total += rb[o - 1]
-    for n in range(BB):
-        o_ref[n] = total[:, n * NA : (n + 1) * NA]
-
     @pl.when(zl == 0)
     def _():
         for s in range(8):
@@ -349,8 +345,16 @@
         left(far_chunk(0, 0), pf_send.at[s])
     for o in range(7):
         left(r0.at[0], ra_send.at[o])
+
     for o in range(15):
         left(rbs.at[0], rb_send.at[o])
+    total = rbs[idx_b]
+    for o in range(1, 16):
+        arrived(rb.at[o - 1], rb_recv.at[o - 1])
+    for o in range(1, 16):
+        total += rb[o - 1]
+    for n in range(BB):
+        o_ref[n] = total[:, n * NA : (n + 1) * NA]
 
 
 def body(factors, amplitudes):
@@ -358,9 +362,10 @@
     return pl.pallas_call(
         kernel,
         out_shape=jax.ShapeDtypeStruct((BB, 1, NA), F32),
-        in_specs=[pl.BlockSpec(memory_space=pltpu.VMEM)] * 2,
+        in_specs=[pl.BlockSpec(memory_space=pl.ANY)] * 2,
         out_specs=pl.BlockSpec(memory_space=pltpu.VMEM),
         scratch_shapes=[
+            pltpu.VMEM((NA, NCV, AUX), BF),
             pltpu.VMEM((8, AUX), BF),
             pltpu.VMEM((16, 4, NC, 8, AUX), BF),
             pltpu.VMEM((NZL, NY, NC, NCV, V), BF),
@@ -373,7 +378,7 @@
             pltpu.VMEM((7, NZH, NY, 128), F32),
             pltpu.VMEM((16, 1, 128), F32),
             pltpu.VMEM((15, 1, 128), F32),
-            dma((2,)), pltpu.SemaphoreType.REGULAR, dma((8,)), dma((2,)), dma((7,)), dma((7,)), dma((3,)), dma((3,)), dma((14,)), dma((14,)), dma((7,)),
+            dma((3,)), pltpu.SemaphoreType.REGULAR, dma((8,)), dma((2,)), dma((7,)), dma((7,)), dma((3,)), dma((3,)), dma((14,)), dma((14,)), dma((7,)),
             dma((7,)), dma((12,)), dma((12,)), dma((8,)), dma((8,)), dma((16,)), dma((16,)), dma((7,)), dma((7,)), dma((15,)), dma((15,)),
         ],
         compiler_params=pltpu.CompilerParams(collective_id=0, has_side_effects=True),

time: 68.4 us -> 67.2 us (0.982)
  Pallas kernels: 66.9 us -> 65.8 us
    pallas_call x1, Pallas kernels: 66.9 us -> 65.8 us  [body(): pl.pallas_call(kernel, out_shape=jax.ShapeDtypeStruct((BB, 1, NA), F32),...]
where the time goes in v4:
time: 67.2 us; the launch traced here: 67.1 us
  Pallas kernels  65.8 us (98%)
  local copies, waits for them, and re-layouts  1.24 us (2%)
    pallas_call x1, Pallas kernels, body(): pl.pallas_call(kernel, out_shape=jax.ShapeDtypeStruct((BB, 1, NA), F32),...  65.8 us

profile of v4, /device:TPU:64, one launch (start us, length us, event | category | flops | bytes accessed | tf_op | source)
XLA Modules:
  0.0 67.1 jit_solution(5667390414958174257)
XLA Ops:
  0.0 65.8 %shard_map.28 = f32[2,1,64]{2,1,0:T(1,128)} custom-call(bf16[64,4,1536]{2,1,0:T(4,128)(2,1)} %f_hbm.1, bf16[8,2,4,512]{3,2,1,0:T(4,128)(2,1)} %bitcast.1), custom_call_target="tpu_custom_call" | custom-call | tf_op jit(solution)/shard_map/pallas_call | solution.py:362
  65.8 1.2 %copy.4 = f32[2,1,64]{2,1,0:T(1,128)} copy(f32[2,1,64]{2,1,0:T(1,128)} %shard_map.28) | data formatting | bytes 1024

commit v5 on v4

--- a/solution.py
+++ b/solution.py
@@ -106,6 +106,9 @@
     def _():
         for s, o in enumerate((4, 3, 2, 1)):
             put(near_own, far_own, z_send.at[s], z_recv.at[1], **at_z(o))
+        arrived(far_own, z_recv.at[1])
+        for s, o in enumerate((-3, -2, -1)):
+            put(far_own, far_own, z_send.at[4 + s], z_recv.at[1], **at_z(o))
 
     for o in range(1, NX):
         put(near_own, near_own, xn_send.at[o - 1], xn_recv.at[o - 1], x=lax.rem(x + o, NX))
@@ -177,12 +180,9 @@
         ring(7, 1, f, down)
     share_near(7)
 
-    arrived(far_own, z_recv.at[1])
-
-    @pl.when(zl == 4)
-    def _():
-        for s, o in enumerate((-3, -2, -1)):
-            put(far_own, far_own, z_send.at[4 + s], z_recv.at[1], **at_z(o))
+    @pl.when(zl != 4)
+    def _():
+        arrived(far_own, z_recv.at[1])
 
     pl.semaphore_wait(mid_sem, 1)
 

time: 67.2 us -> 65.3 us (0.972)
  the two profiles are of different devices: /device:TPU:64 before, /device:TPU:1 now
where the time goes in v5:
time: 65.3 us; the launch traced here: 65.1 us
  Pallas kernels  63.9 us (98%)
  local copies, waits for them, and re-layouts  1.24 us (2%)
    pallas_call x1, Pallas kernels, body(): pl.pallas_call(kernel, out_shape=jax.ShapeDtypeStruct((BB, 1, NA), F32),...  63.9 us

profile of v5, /device:TPU:1, one launch (start us, length us, event | category | flops | bytes accessed | tf_op | source)
XLA Modules:
  0.0 65.1 jit_solution(3116374661931008339)
XLA Ops:
  0.0 63.9 %shard_map.28 = f32[2,1,64]{2,1,0:T(1,128)} custom-call(bf16[64,4,1536]{2,1,0:T(4,128)(2,1)} %f_hbm.1, bf16[8,2,4,512]{3,2,1,0:T(4,128)(2,1)} %bitcast.1), custom_call_target="tpu_custom_call" | custom-call | tf_op jit(solution)/shard_map/pallas_call | solution.py:362
  63.9 1.2 %copy.4 = f32[2,1,64]{2,1,0:T(1,128)} copy(f32[2,1,64]{2,1,0:T(1,128)} %shard_map.28) | data formatting | bytes 1024

commit v6 on v5

--- a/solution.py
+++ b/solution.py
@@ -266,6 +266,9 @@
     near_shared(3)
     multiply(1)
     rows_on(3)
+    near_shared(4)
+    near_shared(5)
+    multiply(2)
     for o in range(4, NZL - 1):
         arrived(t_ref, t_recv.at[o])
     gather_pairs(1 - zl // 4)
@@ -280,9 +283,6 @@
     for m in range(2, 4):
         far_arrived(2, m)
         share_far(2, m)
-    near_shared(4)
-    near_shared(5)
-    multiply(2)
     for k in (1, 3):
         far_shared(k)
         multiply(4 + k)

time: 65.3 us -> 65 us (level)
  no operation moved by 1% of the time
where the time goes in v6:
time: 65 us; the launch traced here: 64.9 us
  Pallas kernels  63.6 us (98%)
  local copies, waits for them, and re-layouts  1.24 us (2%)
    pallas_call x1, Pallas kernels, body(): pl.pallas_call(kernel, out_shape=jax.ShapeDtypeStruct((BB, 1, NA), F32),...  63.6 us

profile of v6, /device:TPU:1, one launch (start us, length us, event | category | flops | bytes accessed | tf_op | source)
XLA Modules:
  0.0 64.9 jit_solution(15386613308227168903)
XLA Ops:
  0.0 63.6 %shard_map.28 = f32[2,1,64]{2,1,0:T(1,128)} custom-call(bf16[64,4,1536]{2,1,0:T(4,128)(2,1)} %f_hbm.1, bf16[8,2,4,512]{3,2,1,0:T(4,128)(2,1)} %bitcast.1), custom_call_target="tpu_custom_call" | custom-call | tf_op jit(solution)/shard_map/pallas_call | solution.py:362
  63.6 1.2 %copy.4 = f32[2,1,64]{2,1,0:T(1,128)} copy(f32[2,1,64]{2,1,0:T(1,128)} %shard_map.28) | data formatting | bytes 1024
